TPU v7x, 32 devices: a whole 2x2x4 slice. The times are simulated.
32 devices in a mesh: dp: 8 (over z, x), tensor: 4 (over y, core).
Axes of the slice: x: 2, y: 2, z: 4, core: 2. Of those that a mesh axis runs over, the one named last changes fastest.
Arguments:
- inputs: bfloat16 [2048, 8192], P('dp', 'tensor'), may hold values from -6 to 6
- out_grads: bfloat16 [2048, 8192], P('dp', 'tensor'), may hold values from -6 to 6
- gate_pre: bfloat16 [2048, 28672], P('dp', 'tensor'), may hold values from -6 to 6
- up_pre: bfloat16 [2048, 28672], P('dp', 'tensor'), may hold values from -6 to 6
- hidden_grad: bfloat16 [2048, 28672], P('dp', 'tensor'), may hold values from -6 to 6
- proj_model: bfloat16 [8192, 128], P(('tensor', 'dp')), may hold values from -0.0625 to 0.0625
- proj_hidden: bfloat16 [28672, 192], P(('tensor', 'dp')), may hold values from -0.03125 to 0.03125
- lengths: int32 [8, 4], P('dp'), may hold values from 1 to 192, 256 in all within a row
- owners: int32 [8, 4], P('dp'), may hold values from 0 to 3, each once within a row
Outputs:
- features: float32 [32, 12288], P(('dp', 'tensor'))
Inputs may be any that keep to these rules, and one draw needn't show every extreme that they name: `lengths`: each row sums to 256, and each row has an example of exactly 192 tokens. `owners`: each row names every slot once.
All inputs are finite; a program needn't handle non-finite values.
Results may differ from a plain program's by a relative error of at most 0.0029.
Values may be sent and summed in bfloat16 or wider, within the bound.
A program may use at most 64 MiB of HBM per device.

v0:
```python
import jax
import jax.numpy as jnp
from jax import lax
from jax.sharding import PartitionSpec as P


def per_device(
    inputs, out_grads, gate_pre, up_pre, hidden_grad, proj_model, proj_hidden, lengths, owners
):
    rank_width = proj_model.shape[1] // 2
    tok_rows = inputs.shape[0]
    gate_value = gate_pre.astype(jnp.float32)
    up_value = up_pre.astype(jnp.float32)
    grad_value = hidden_grad.astype(jnp.float32)
    sigmoid_gate = jax.nn.sigmoid(gate_value)
    hidden = (gate_value * sigmoid_gate * up_value).astype(jnp.bfloat16)
    up_grad = (grad_value * gate_value * sigmoid_gate).astype(jnp.bfloat16)
    gate_grad = (
        grad_value * up_value * sigmoid_gate * (1.0 + gate_value * (1.0 - sigmoid_gate))
    ).astype(jnp.bfloat16)
    sources = (gate_grad, up_grad, hidden)
    block_rows = lax.all_gather(proj_hidden, "dp", axis=0, tiled=True)
    parts = []
    for column, source in enumerate(sources):
        parts.append(
            jnp.dot(
                source,
                block_rows[:, column * rank_width : (column + 1) * rank_width],
                preferred_element_type=jnp.float32,
            )
        )
    hidden_part = jnp.concatenate(parts, axis=1)
    block_rows = lax.all_gather(proj_model, "dp", axis=0, tiled=True)
    first_part = jnp.dot(inputs, block_rows[:, :rank_width], preferred_element_type=jnp.float32)
    second_part = jnp.dot(out_grads, block_rows[:, rank_width:], preferred_element_type=jnp.float32)
    model_part = jnp.concatenate([first_part, second_part], axis=1)
    partial_value = jnp.concatenate([hidden_part, model_part], axis=1)
    lens = lengths[0]
    owner_row = owners[0]
    starts = jnp.cumsum(lens) - lens
    myself = lax.axis_index("tensor")
    tensor_count = lax.axis_size("tensor")
    chosen = (owner_row == myself).astype(jnp.int32)
    my_length = jnp.sum(lens * chosen)
    capacity = 3 * tok_rows // tensor_count
    slots = jnp.arange(capacity * lax.axis_size("tensor"), dtype=jnp.int32)
    holder = slots // capacity
    within = slots % capacity
    matched = (owner_row[None, :] == holder[:, None]).astype(jnp.int32)
    first_token = jnp.sum(matched * starts[None, :], axis=1)
    span = jnp.sum(matched * lens[None, :], axis=1)
    valid = within < span
    picked = jnp.where(valid, first_token + within, 0)
    summed = lax.psum_scatter(
        jnp.take(partial_value, picked, axis=0) * valid[:, None].astype(jnp.float32),
        "tensor",
        scatter_dimension=0,
        tiled=True,
    )
    weights = (jnp.arange(capacity, dtype=jnp.int32) < my_length).astype(jnp.float32)

    def block_of(index):
        return summed[:, index * rank_width : (index + 1) * rank_width]

    pairs = ((0, 3), (1, 3), (4, 2))
    blocks = []
    for left_index, right_index in pairs:
        left_side = block_of(left_index) * weights[:, None]
        blocks.append(
            jnp.einsum(
                "ta,tb->ab", left_side, block_of(right_index), precision=lax.Precision.HIGHEST
            )
        )
    return jnp.stack(blocks, axis=0).reshape(1, 3 * rank_width * rank_width)


def solution(mesh):
    in_specs = (
        P("dp", "tensor"),
        P("dp", "tensor"),
        P("dp", "tensor"),
        P("dp", "tensor"),
        P("dp", "tensor"),
        P(("tensor", "dp"), None),
        P(("tensor", "dp"), None),
        P("dp", None),
        P("dp", None),
    )
    out_specs = P(("dp", "tensor"), None)
    return jax.shard_map(
        per_device, mesh=mesh, in_specs=in_specs, out_specs=out_specs, check_vma=False
    )
```

profile of v0, /device:TPU:0, one launch (start us, length us, event | category | flops | bytes accessed | tf_op | source)
XLA Modules:
  0.0 123.5 jit_solution(9361023392948454162)
XLA Ops:
  6.5 0.7 all-gather.2.cloned.1.call-update
  7.3 0.0 reduce-scatter.2.cloned.1.call-start
  7.3 0.8 reduce-window_clone.1
  8.1 0.7 subtract_bitcast_fusion
  8.8 0.8 fusion.36
  9.6 34.1 %all_gather.7 = bf16[2048,128]{1,0:T(8,128)(2,1)S(1)} all-gather(bf16[256,128]{1,0:T(8,128)(2,1)} %param.14), channel_id=1, replica_groups=mesh['dp'=8,'tensor'=4] {'dp'}, dimensions={0}, use_global_device_ids=true | all-gather | bytes 589824 | tf_op jit(solution)/shard_map/all_gather | solution.py:33
  43.8 26.8 %all-gather.2.cloned.1.call-done = bf16[7168,192]{0,1:T(8,128)(2,1)} async-done(((bf16[896,192]{0,1:T(8,128)(2,1)}), bf16[7168,192]{0,1:T(8,128)(2,1)}) %all-gather.2.cloned.1.call-update) | async-done | bytes 2752528 | tf_op jit(solution)/shard_map/all_gather | solution.py:22
  70.6 7.6 %fusion.16 = f32[256,320]{0,1:T(8,128)S(1)} fusion(bf16[256,7168]{1,0:T(8,128)(2,1)} %param.12, bf16[256,7168]{1,0:T(8,128)(2,1)} %param.13, bf16[256,7168]{1,0:T(8,128)(2,1)} %param.11, bf16[7168,192]{0,1:T(8,128)(2,1)} %all-gather.2.cloned.1.call-done), kind=kOutput, calls=%fused_computation.23 | convolution fusion | flops 258736128 | bytes 11993088 | tf_op jit(solution)/shard_map/dot_general | solution.py:26
  78.2 0.0 copy-start.5
  78.2 2.2 %fusion.22 = f32[256,320]{0,1:T(8,128)S(1)} fusion(f32[256,320]{0,1:T(8,128)S(1)} %fusion.16, bf16[256,7168]{1,0:T(8,128)(2,1)S(1)} %copy-done.6, bf16[256,7168]{1,0:T(8,128)(2,1)S(1)} %copy-done.4, bf16[7168,192]{0,1:T(8,128)(2,1)S(1)} %copy-done.7), kind=kOutput, calls=%fused_computation.25 | convolution fusion | flops 249561088 | bytes 8323072 | tf_op jit(solution)/shard_map/dot_general | solution.py:26
  80.5 2.3 %fusion.19 = f32[256,320]{0,1:T(8,128)S(1)} fusion(f32[256,320]{0,1:T(8,128)S(1)} %fusion.22, bf16[256,7168]{1,0:T(8,128)(2,1)S(1)} %copy-done.5, bf16[256,7168]{1,0:T(8,128)(2,1)S(1)} %copy-done.6, bf16[7168,192]{0,1:T(8,128)(2,1)S(1)} %copy-done.7), kind=kOutput, calls=%fused_computation.24 | convolution fusion | flops 249561088 | bytes 8323072 | tf_op jit(solution)/shard_map/dot_general | solution.py:26
  82.8 0.5 convolution_dynamic-update-slice_fusion.1
  83.3 0.6 convolution_dynamic-update-slice_fusion
  83.9 0.2 copy.12
  84.1 2.1 %gather_fusion = f32[768,320]{1,0:T(8,128)S(1)} fusion(f32[256,320]{1,0:T(8,128)S(1)} %copy.12, s32[1024]{0:T(1024)S(1)} %pad_clamp_fusion), kind=kCustom, calls=%fused_computation | custom fusion | bytes 1969152 | tf_op jit(solution)/shard_map/jit(_take)/gather | solution.py:55
  86.2 1.3 %select_multiply_fusion = f32[768,320]{1,0:T(8,128)} fusion(f32[768,320]{1,0:T(8,128)S(1)} %gather_fusion, f32[768]{0:T(1024)S(1)} %convert_element_type.41, pred[768]{0:T(1024)(128)(4,1)S(1)} %get-tuple-element.7), kind=kLoop, calls=%fused_computation.20 | loop fusion | flops 491520 | bytes 1969920 | tf_op jit(solution)/shard_map/mul | solution.py:55
  87.5 0.0 reduce-scatter.2.cloned.1.call-update
  87.6 0.6 fusion.45
  88.2 0.6 compare_convert_fusion
  88.9 22.9 %reduce-scatter.2.cloned.1.call-done = f32[192,320]{1,0:T(8,128)} async-done(((f32[768,320]{1,0:T(8,128)}), f32[192,320]{1,0:T(8,128)}) %reduce-scatter.2.cloned.1.call-update) | async-done | bytes 245776 | tf_op jit(solution)/shard_map/reduce_scatter | solution.py:54
  111.8 1.3 %convolution_bitcast_fusion = f32[1,64,64]{2,1,0:T(8,128)S(1)} fusion(f32[192,320]{1,0:T(8,128)} %reduce-scatter.2.cloned.1.call-done, f32[192]{0:T(256)S(1)} %compare_convert_fusion), kind=kOutput, calls=%fused_computation.26 | convolution fusion | flops 9449472 | bytes 213760 | tf_op jit(solution)/shard_map/ta,tb->ab/dot_general | solution.py:70
  113.1 1.4 %convolution_bitcast_fusion.1 = f32[1,64,64]{2,1,0:T(8,128)S(1)} fusion(f32[192,320]{1,0:T(8,128)} %reduce-scatter.2.cloned.1.call-done, f32[192]{0:T(256)S(1)} %compare_convert_fusion), kind=kOutput, calls=%fused_computation.27 | convolution fusion | flops 9449472 | bytes 213760 | tf_op jit(solution)/shard_map/ta,tb->ab/dot_general | solution.py:70
  114.5 1.3 %convolution_bitcast_fusion.2 = f32[1,64,64]{2,1,0:T(8,128)S(1)} fusion(f32[192,320]{1,0:T(8,128)} %reduce-scatter.2.cloned.1.call-done, f32[192]{0:T(256)S(1)} %compare_convert_fusion), kind=kOutput, calls=%fused_computation.28 | convolution fusion | flops 9449472 | bytes 213760 | tf_op jit(solution)/shard_map/ta,tb->ab/dot_general | solution.py:70
  115.9 0.7 reshape.85
  (22 shorter events, 0.1 us)
Async XLA Ops:
  6.5 76.2 %copy-start = (bf16[256,2048]{1,0:T(8,128)(2,1)S(1)}, bf16[256,2048]{1,0:T(8,128)(2,1)}, u32[]{:S(2)}) copy-start(bf16[256,2048]{1,0:T(8,128)(2,1)} %param.9) | copy-start | bytes 3145732
  6.5 64.1 %all-gather.2.cloned.1.call-start = ((), (), s32[]{:S(2)}) async-start(), calls=%async_computation.1 | async-start | bytes 3096576 | tf_op jit(solution)/shard_map/all_gather | solution.py:22
  7.3 104.5 %reduce-scatter.2.cloned.1.call-start = ((), (), s32[]{:S(2)}) async-start(), calls=%async_computation.2 | async-start | bytes 1474560 | tf_op jit(solution)/shard_map/reduce_scatter | solution.py:54
  70.6 7.6 %copy-start.4 = (bf16[256,7168]{1,0:T(8,128)(2,1)S(1)}, bf16[256,7168]{1,0:T(8,128)(2,1)}, u32[]{:S(2)}) copy-start(bf16[256,7168]{1,0:T(8,128)(2,1)} %param.13) | copy-start | bytes 11010052
  70.6 7.6 %copy-start.6 = (bf16[256,7168]{1,0:T(8,128)(2,1)S(1)}, bf16[256,7168]{1,0:T(8,128)(2,1)}, u32[]{:S(2)}) copy-start(bf16[256,7168]{1,0:T(8,128)(2,1)} %param.11) | copy-start | bytes 11010052
  70.6 7.6 %copy-start.7 = (bf16[7168,192]{0,1:T(8,128)(2,1)S(1)}, bf16[7168,192]{0,1:T(8,128)(2,1)}, u32[]{:S(2)}) copy-start(bf16[7168,192]{0,1:T(8,128)(2,1)} %all-gather.2.cloned.1.call-done) | copy-start | bytes 8257540
  78.2 2.3 %copy-start.5 = (bf16[256,7168]{1,0:T(8,128)(2,1)S(1)}, bf16[256,7168]{1,0:T(8,128)(2,1)}, u32[]{:S(2)}) copy-start(bf16[256,7168]{1,0:T(8,128)(2,1)} %param.12) | copy-start | bytes 11010052
  80.5 2.8 %copy-start.1 = (bf16[256,2048]{1,0:T(8,128)(2,1)S(1)}, bf16[256,2048]{1,0:T(8,128)(2,1)}, u32[]{:S(2)}) copy-start(bf16[256,2048]{1,0:T(8,128)(2,1)} %param.10) | copy-start | bytes 3145732
  84.1 3.5 %copy-start.2 = (s32[1,4]{1,0:T(1,128)S(1)}, s32[1,4]{1,0:T(1,128)}, u32[]{:S(2)}) copy-start(s32[1,4]{1,0:T(1,128)} %param.16) | copy-start | bytes 52
  84.1 3.5 %copy-start.3 = (s32[1,4]{1,0:T(1,128)S(1)}, s32[1,4]{1,0:T(1,128)}, u32[]{:S(2)}) copy-start(s32[1,4]{1,0:T(1,128)} %param.17) | copy-start | bytes 52
Sparse Core Ops, SparseCore 0:
  9.5 61.0 all-gather.1
  87.7 24.0 reduce-scatter.1
where the time goes:
time: 124 us; the launch traced here: 123 us
  waiting for transfers between devices  50.5 us (41%)
  blocking collectives  34.1 us (28%)
  matrix products  17.3 us (14%)
  between operations  13.6 us (11%)
  other arithmetic  4.88 us (4%)
  local copies, waits for them, and re-layouts  3.07 us (2%)
    all_gather x1, blocking collectives, per_device(): block_rows = lax.all_gather(proj_model, 'dp', axis=0, tiled=True)  34.1 us
    all_gather x1, waiting for transfers between devices, per_device(): block_rows = lax.all_gather(proj_hidden, 'dp', axis=0, tiled=True)  26.8 us
    reduce_scatter x1, waiting for transfers between devices, per_device(): lax.psum_scatter(jnp.take(partial_value, picked, axis=0) * valid[:, None]...  22.9 us
    dot_general x3, matrix products, per_device(): jnp.dot(source, block_rows[:, column * rank_width:(column + 1) * rank_wid...  12.1 us
    dot_general x3, matrix products, per_device(): jnp.einsum('ta,tb->ab', left_side, block_of(right_index), precision=lax.P...  4.07 us
  transfers between devices with their start and end apart: 2, of which 2 were waited for; matrix products, arithmetic and copies ran while one was open for 3% of the time, Pallas kernels for 0%

commit v1 on v0

--- a/solution.py
+++ b/solution.py
@@ -19,7 +19,12 @@
         grad_value * up_value * sigmoid_gate * (1.0 + gate_value * (1.0 - sigmoid_gate))
     ).astype(jnp.bfloat16)
     sources = (gate_grad, up_grad, hidden)
-    block_rows = lax.all_gather(proj_hidden, "dp", axis=0, tiled=True)
+    ring = [proj_hidden]
+    for hop in range(7):
+        ring.append(lax.ppermute(ring[-1], "dp", [(dev, (dev + 1) % 8) for dev in range(8)]))
+    block_rows = jnp.roll(
+        jnp.concatenate(ring[::-1], axis=0), (lax.axis_index("dp") + 1) * ring[0].shape[0], axis=0
+    )
     parts = []
     for column, source in enumerate(sources):
         parts.append(

time: 124 us -> 163 us (1.31)
  waiting for transfers between devices: 50.5 us -> 85.4 us
  local copies, waits for them, and re-layouts: 3.07 us -> 6.61 us
  matrix products: 17.3 us -> 14.2 us
  starting transfers between devices: 0.04 us -> 2.96 us
    ppermute x0 -> x7, waiting for transfers between devices: none -> 62.5 us  [per_device(): lax.ppermute(ring[-1], 'dp', [(dev, (dev + 1) % 8) for dev in range(8)])]
    all_gather x1 -> x0, waiting for transfers between devices: 26.8 us -> none  [per_device(): block_rows = lax.all_gather(proj_hidden, 'dp', axis=0, tiled=True)]
    unnamed x16 -> x31, local copies, waits for them, and re-layouts: 0.04 us -> 3.53 us
    dot_general x3, matrix products: 12.1 us -> 8.99 us  [per_device(): jnp.dot(source, block_rows[:, column * rank_width:(column + 1) * rank_wid...]
    ppermute x0 -> x7, starting transfers between devices: none -> 2.95 us  [per_device(): lax.ppermute(ring[-1], 'dp', [(dev, (dev + 1) % 8) for dev in range(8)])]
  transfers between devices with their start and end apart: 2 -> 8, of which waited for: 2 -> 7; matrix products, arithmetic and copies ran while one was open for 3% -> 2% of each run, Pallas kernels for 0% -> 0%
where the time goes in v1:
time: 163 us; the launch traced here: 162 us
  waiting for transfers between devices  85.4 us (52%)
  blocking collectives  34.7 us (21%)
  matrix products  14.2 us (9%)
  between operations  13.7 us (8%)
  local copies, waits for them, and re-layouts  6.61 us (4%)
  other arithmetic  4.89 us (3%)
  starting transfers between devices  2.96 us (2%)
    ppermute x7, waiting for transfers between devices, per_device(): lax.ppermute(ring[-1], 'dp', [(dev, (dev + 1) % 8) for dev in range(8)])  62.5 us
    all_gather x1, blocking collectives, per_device(): block_rows = lax.all_gather(proj_model, 'dp', axis=0, tiled=True)  34.7 us
    reduce_scatter x1, waiting for transfers between devices, per_device(): lax.psum_scatter(jnp.take(partial_value, picked, axis=0) * valid[:, None]...  22.9 us
    dot_general x3, matrix products, per_device(): jnp.dot(source, block_rows[:, column * rank_width:(column + 1) * rank_wid...  8.99 us
    dot_general x3, matrix products, per_device(): jnp.einsum('ta,tb->ab', left_side, block_of(right_index), precision=lax.P...  4.07 us
    unnamed x31, local copies, waits for them, and re-layouts  3.53 us
  transfers between devices with their start and end apart: 8, of which 7 were waited for; matrix products, arithmetic and copies ran while one was open for 2% of the time, Pallas kernels for 0%

profile of v1, /device:TPU:0, one launch (start us, length us, event | category | flops | bytes accessed | tf_op | source)
XLA Modules:
  0.0 162.4 jit_solution(4607878466463320096)
XLA Ops:
  6.5 2.9 %collective-permute-start = (bf16[896,192]{0,1:T(8,128)(2,1)}, bf16[896,192]{0,1:T(8,128)(2,1)S(1)}, u32[]{:S(2)}, u32[]{:S(2)}) collective-permute-start(bf16[896,192]{0,1:T(8,128)(2,1)} %param.15), channel_id=1, source_target_pairs={{0,4},{4,8},{8,12},{12,16},{16,20},{20,24},{24,28},{28,0},{1,5},{5... | collective-permute-start | bytes 1032200 | tf_op jit(solution)/shard_map/ppermute | solution.py:24
  9.5 11.3 %collective-permute-done = bf16[896,192]{0,1:T(8,128)(2,1)S(1)} collective-permute-done((bf16[896,192]{0,1:T(8,128)(2,1)}, bf16[896,192]{0,1:T(8,128)(2,1)S(1)}, u32[]{:S(2)}, u32[]{:S(2)}) %collective-permute-start) | collective-permute-done | bytes 344096 | tf_op jit(solution)/shard_map/ppermute | solution.py:24
  20.8 11.9 %collective-permute-done.1 = bf16[896,192]{0,1:T(8,128)(2,1)S(1)} collective-permute-done((bf16[896,192]{0,1:T(8,128)(2,1)S(1)}, bf16[896,192]{0,1:T(8,128)(2,1)S(1)}, u32[]{:S(2)}, u32[]{:S(2)}) %collective-permute-start.1) | collective-permute-done | bytes 344096 | tf_op jit(solution)/shard_map/ppermute | solution.py:24
  32.8 11.0 %collective-permute-done.2 = bf16[896,192]{0,1:T(8,128)(2,1)S(1)} collective-permute-done((bf16[896,192]{0,1:T(8,128)(2,1)S(1)}, bf16[896,192]{0,1:T(8,128)(2,1)S(1)}, u32[]{:S(2)}, u32[]{:S(2)}) %collective-permute-start.2) | collective-permute-done | bytes 344096 | tf_op jit(solution)/shard_map/ppermute | solution.py:24
  43.8 10.1 %collective-permute-done.3 = bf16[896,192]{0,1:T(8,128)(2,1)S(1)} collective-permute-done((bf16[896,192]{0,1:T(8,128)(2,1)S(1)}, bf16[896,192]{0,1:T(8,128)(2,1)S(1)}, u32[]{:S(2)}, u32[]{:S(2)}) %collective-permute-start.3) | collective-permute-done | bytes 344096 | tf_op jit(solution)/shard_map/ppermute | solution.py:24
  53.9 0.8 reduce-window_clone.1
  54.7 0.7 subtract_bitcast_fusion
  55.4 8.5 %collective-permute-done.4 = bf16[896,192]{0,1:T(8,128)(2,1)S(1)} collective-permute-done((bf16[896,192]{0,1:T(8,128)(2,1)S(1)}, bf16[896,192]{0,1:T(8,128)(2,1)S(1)}, u32[]{:S(2)}, u32[]{:S(2)}) %collective-permute-start.4) | collective-permute-done | bytes 344096 | tf_op jit(solution)/shard_map/ppermute | solution.py:24
  63.9 0.8 fusion.36
  64.7 9.6 %collective-permute-done.5 = bf16[896,192]{0,1:T(8,128)(2,1)S(1)} collective-permute-done((bf16[896,192]{0,1:T(8,128)(2,1)S(1)}, bf16[896,192]{0,1:T(8,128)(2,1)S(1)}, u32[]{:S(2)}, u32[]{:S(2)}) %collective-permute-start.5) | collective-permute-done | bytes 344096 | tf_op jit(solution)/shard_map/ppermute | solution.py:24
  74.4 34.7 %all_gather.3 = bf16[2048,128]{1,0:T(8,128)(2,1)S(1)} all-gather(bf16[256,128]{1,0:T(8,128)(2,1)} %param.14), channel_id=1, replica_groups=mesh['dp'=8,'tensor'=4] {'dp'}, dimensions={0}, use_global_device_ids=true | all-gather | bytes 589824 | tf_op jit(solution)/shard_map/all_gather | solution.py:38
  109.1 1.2 constant_dynamic-update-slice_fusion.15
  110.7 1.7 %constant_dynamic-update-slice_fusion.7 = bf16[14336,192]{0,1:T(8,128)(2,1)S(1)} fusion(bf16[14336,192]{0,1:T(8,128)(2,1)S(1)} %constant_dynamic-update-slice_fusion.8, bf16[896,192]{0,1:T(8,128)(2,1)} %collective-permute-done.6), kind=kLoop, calls=%fused_computation.51 | loop fusion | bytes 688128
  112.8 3.7 %fusion.16 = f32[256,320]{0,1:T(8,128)S(1)} fusion(bf16[256,7168]{1,0:T(8,128)(2,1)S(1)} %copy-done.6, bf16[256,7168]{1,0:T(8,128)(2,1)S(1)} %copy-done.5, bf16[256,7168]{1,0:T(8,128)(2,1)S(1)} %copy-done.7, bf16[14336,192]{0,1:T(8,128)(2,1)S(1)} %constant_dynamic-update-slice_fusion, s32[]{:T(128)S(6)} %select_n.85), kind=kOutput, calls=%fused_computation.23 | convolution fusion | flops 258736128 | bytes 11993092 | tf_op jit(solution)/shard_map/dot_general | solution.py:31
  116.5 2.5 %fusion.22 = f32[256,320]{0,1:T(8,128)S(1)} fusion(f32[256,320]{0,1:T(8,128)S(1)} %fusion.16, bf16[256,7168]{1,0:T(8,128)(2,1)S(1)} %copy-done.7, bf16[256,7168]{1,0:T(8,128)(2,1)S(1)} %copy-done.5, bf16[14336,192]{0,1:T(8,128)(2,1)S(1)} %constant_dynamic-update-slice_fusion, s32[]{:T(128)S(6)} %select_n.85, s32[]{:T(128)S(6)} %add.99), kind=kOutput, calls=%fused_computation.25 | convolution fusion | flops 249561088 | bytes 8323080 | tf_op jit(solution)/shard_map/dot_general | solution.py:31
  119.1 2.7 %fusion.19 = f32[256,320]{0,1:T(8,128)S(1)} fusion(f32[256,320]{0,1:T(8,128)S(1)} %fusion.22, bf16[256,7168]{1,0:T(8,128)(2,1)S(1)} %copy-done.6, bf16[256,7168]{1,0:T(8,128)(2,1)S(1)} %copy-done.7, bf16[14336,192]{0,1:T(8,128)(2,1)S(1)} %constant_dynamic-update-slice_fusion, s32[]{:T(128)S(6)} %select_n.85, s32[]{:T(128)S(6)} %add.100), kind=kOutput, calls=%fused_computation.24 | convolution fusion | flops 249561088 | bytes 8323080 | tf_op jit(solution)/shard_map/dot_general | solution.py:31
  123.1 2.1 %gather_fusion = f32[768,320]{1,0:T(8,128)S(1)} fusion(f32[256,320]{1,0:T(8,128)S(1)} %copy.12, s32[1024]{0:T(1024)S(1)} %pad_clamp_fusion), kind=kCustom, calls=%fused_computation | custom fusion | bytes 1969152 | tf_op jit(solution)/shard_map/jit(_take)/gather | solution.py:60
  125.2 1.3 select_multiply_fusion
  127.2 0.6 compare_convert_fusion
  127.9 22.9 %reduce-scatter.2.cloned.1.call-done = f32[192,320]{1,0:T(8,128)} async-done(((f32[768,320]{1,0:T(8,128)}), f32[192,320]{1,0:T(8,128)}) %reduce-scatter.2.cloned.1.call-update) | async-done | bytes 245776 | tf_op jit(solution)/shard_map/reduce_scatter | solution.py:59
  150.7 1.4 convolution_bitcast_fusion.1
  152.1 1.3 convolution_bitcast_fusion.2
  153.4 1.4 convolution_bitcast_fusion
  154.8 0.7 reshape.85
  (49 shorter events, 2.7 us)
Async XLA Ops:
  6.5 115.3 %copy-start = (bf16[256,2048]{1,0:T(8,128)(2,1)S(1)}, bf16[256,2048]{1,0:T(8,128)(2,1)}, u32[]{:S(2)}) copy-start(bf16[256,2048]{1,0:T(8,128)(2,1)} %param.9) | copy-start | bytes 3145732
  6.5 104.1 %copy-start.1 = (bf16[896,192]{0,1:T(8,128)(2,1)S(1)}, bf16[896,192]{0,1:T(8,128)(2,1)}, u32[]{:S(2)}) copy-start(bf16[896,192]{0,1:T(8,128)(2,1)} %param.15) | copy-start | bytes 1032196
  6.5 144.2 %reduce-scatter.2.cloned.1.call-start = ((), (), s32[]{:S(2)}) async-start(), calls=%async_computation.1 | async-start | bytes 1474560 | tf_op jit(solution)/shard_map/reduce_scatter | solution.py:59
  6.5 14.3 %collective-permute-start = (bf16[896,192]{0,1:T(8,128)(2,1)}, bf16[896,192]{0,1:T(8,128)(2,1)S(1)}, u32[]{:S(2)}, u32[]{:S(2)}) collective-permute-start(bf16[896,192]{0,1:T(8,128)(2,1)} %param.15), channel_id=1, source_target_pairs={{0,4},{4,8},{8,12},{12,16},{16,20},{20,24},{24,28},{28,0},{1,5},{5... | collective-permute-start | bytes 1032200 | tf_op jit(solution)/shard_map/ppermute | solution.py:24
  20.8 11.9 %collective-permute-start.1 = (bf16[896,192]{0,1:T(8,128)(2,1)S(1)}, bf16[896,192]{0,1:T(8,128)(2,1)S(1)}, u32[]{:S(2)}, u32[]{:S(2)}) collective-permute-start(bf16[896,192]{0,1:T(8,128)(2,1)S(1)} %collective-permute-done), channel_id=1, source_target_pairs={{0,4},{4,8},{8,12},{12,16},{16,20},{20,24},{24,28},{28,0},{1,5},{5... | collective-permute-start | bytes 1032200 | tf_op jit(solution)/shard_map/ppermute | solution.py:24
  32.8 11.0 %collective-permute-start.2 = (bf16[896,192]{0,1:T(8,128)(2,1)S(1)}, bf16[896,192]{0,1:T(8,128)(2,1)S(1)}, u32[]{:S(2)}, u32[]{:S(2)}) collective-permute-start(bf16[896,192]{0,1:T(8,128)(2,1)S(1)} %collective-permute-done.1), channel_id=1, source_target_pairs={{0,4},{4,8},{8,12},{12,16},{16,20},{20,24},{24,28},{28,0},{1,5},{5... | collective-permute-start | bytes 1032200 | tf_op jit(solution)/shard_map/ppermute | solution.py:24
  43.8 10.1 %collective-permute-start.3 = (bf16[896,192]{0,1:T(8,128)(2,1)S(1)}, bf16[896,192]{0,1:T(8,128)(2,1)S(1)}, u32[]{:S(2)}, u32[]{:S(2)}) collective-permute-start(bf16[896,192]{0,1:T(8,128)(2,1)S(1)} %collective-permute-done.2), channel_id=1, source_target_pairs={{0,4},{4,8},{8,12},{12,16},{16,20},{20,24},{24,28},{28,0},{1,5},{5... | collective-permute-start | bytes 1032200 | tf_op jit(solution)/shard_map/ppermute | solution.py:24
  53.9 9.9 %collective-permute-start.4 = (bf16[896,192]{0,1:T(8,128)(2,1)S(1)}, bf16[896,192]{0,1:T(8,128)(2,1)S(1)}, u32[]{:S(2)}, u32[]{:S(2)}) collective-permute-start(bf16[896,192]{0,1:T(8,128)(2,1)S(1)} %collective-permute-done.3), channel_id=1, source_target_pairs={{0,4},{4,8},{8,12},{12,16},{16,20},{20,24},{24,28},{28,0},{1,5},{5... | collective-permute-start | bytes 1032200 | tf_op jit(solution)/shard_map/ppermute | solution.py:24
  63.8 10.5 %collective-permute-start.5 = (bf16[896,192]{0,1:T(8,128)(2,1)S(1)}, bf16[896,192]{0,1:T(8,128)(2,1)S(1)}, u32[]{:S(2)}, u32[]{:S(2)}) collective-permute-start(bf16[896,192]{0,1:T(8,128)(2,1)S(1)} %collective-permute-done.4), channel_id=1, source_target_pairs={{0,4},{4,8},{8,12},{12,16},{16,20},{20,24},{24,28},{28,0},{1,5},{5... | collective-permute-start | bytes 1032200 | tf_op jit(solution)/shard_map/ppermute | solution.py:24
  74.3 34.8 %collective-permute-start.6 = (bf16[896,192]{0,1:T(8,128)(2,1)S(1)}, bf16[896,192]{0,1:T(8,128)(2,1)}, u32[]{:S(2)}, u32[]{:S(2)}) collective-permute-start(bf16[896,192]{0,1:T(8,128)(2,1)S(1)} %collective-permute-done.5), channel_id=1, source_target_pairs={{0,4},{4,8},{8,12},{12,16},{16,20},{20,24},{24,28},{28,0},{1,5},{5... | collective-permute-start | bytes 1032200 | tf_op jit(solution)/shard_map/ppermute | solution.py:24
  74.4 38.4 %copy-start.7 = (bf16[256,7168]{1,0:T(8,128)(2,1)S(1)}, bf16[256,7168]{1,0:T(8,128)(2,1)}, u32[]{:S(2)}) copy-start(bf16[256,7168]{1,0:T(8,128)(2,1)} %param.11) | copy-start | bytes 11010052
  109.1 3.7 %copy-start.5 = (bf16[256,7168]{1,0:T(8,128)(2,1)S(1)}, bf16[256,7168]{1,0:T(8,128)(2,1)}, u32[]{:S(2)}) copy-start(bf16[256,7168]{1,0:T(8,128)(2,1)} %param.13) | copy-start | bytes 11010052
  109.1 3.7 %copy-start.6 = (bf16[256,7168]{1,0:T(8,128)(2,1)S(1)}, bf16[256,7168]{1,0:T(8,128)(2,1)}, u32[]{:S(2)}) copy-start(bf16[256,7168]{1,0:T(8,128)(2,1)} %param.12) | copy-start | bytes 11010052
  119.1 3.2 %copy-start.2 = (bf16[256,2048]{1,0:T(8,128)(2,1)S(1)}, bf16[256,2048]{1,0:T(8,128)(2,1)}, u32[]{:S(2)}) copy-start(bf16[256,2048]{1,0:T(8,128)(2,1)} %param.10) | copy-start | bytes 3145732
  123.1 3.5 %copy-start.3 = (s32[1,4]{1,0:T(1,128)S(1)}, s32[1,4]{1,0:T(1,128)}, u32[]{:S(2)}) copy-start(s32[1,4]{1,0:T(1,128)} %param.16) | copy-start | bytes 52
  123.1 3.5 %copy-start.4 = (s32[1,4]{1,0:T(1,128)S(1)}, s32[1,4]{1,0:T(1,128)}, u32[]{:S(2)}) copy-start(s32[1,4]{1,0:T(1,128)} %param.17) | copy-start | bytes 52
Sparse Core Ops, SparseCore 0:
  126.7 23.9 reduce-scatter.1
